TPU v7x, 256 devices: a whole 4x4x8 slice. The times are simulated.
256 devices in a mesh: det: 64 (over x, z, core), head: 4 (over y).
Axes of the slice: x: 4, y: 4, z: 8, core: 2. Of those that a mesh axis runs over, the one named last changes fastest.
Arguments:
- elements: bfloat16 [32768, 1024], P('det'), may hold values from -6 to 6
- element_types: int32 [32768], P('det'), may hold values from 0 to 1, as said below
- handover_counts: int32 [64, 64], replicated, may hold values from 0 to 16, as said below
- block_lists: int32 [256, 16], P('det'), may hold values from 0 to 255, as said below
- w_first: bfloat16 [2, 1024, 2048], P(None, None, 'head'), may hold values from -0.1875 to 0.1875
- w_second: bfloat16 [2, 2048, 1024], P(None, 'head'), may hold values from -0.125 to 0.125
- w_query: bfloat16 [1024, 1024], P(None, 'head'), may hold values from -3 to 3
- key_value_weight: bfloat16 [1024, 2, 256], P(None, None, 'head'), may hold values from -0.1875 to 0.1875
- attention_cotangent: bfloat16 [32768, 1024], P('det', 'head'), may hold values from -6 to 6
Outputs:
- attended: bfloat16 [32768, 1024], P('det', 'head')
- x_grad: bfloat16 [32768, 1024], P('det', 'head')
Inputs may be any that keep to these rules, and one draw needn't show every extreme that they name: `element_types`: of the 512 elements of each device of det, exactly 256 are of each type. `handover_counts`: row d, column e counts the elements that device d of det hands to device e; every row and every column sums to 512; some entries equal 16. `block_lists`: key block k is held by device k // 4 of det; the 16 entries of a query block may repeat; the lists of the 4 query blocks of one device together name exactly 1 block, counted with repeats, held by each device of det.
All inputs are finite; a program needn't handle non-finite values.
Results may differ from a plain program's by a relative error of at most 0.024.
The roundings to bfloat16 on the way count: a program that leaves them out, or rounds other values in their place, can miss the bound.
Values may be sent and summed in bfloat16 or wider, within the bound.
A program may use at most 64 MiB of HBM per device.

v0:
```python
import jax
import jax.numpy as jnp
from jax import lax
from jax.sharding import PartitionSpec as P

HEAD_SIZE = 64
BLOCK_ROWS = 128
LISTED_COUNT = 16
GROUP_HEADS = 4


def exclusive(counts, reduce_axis):
    return jnp.cumsum(counts, axis=reduce_axis, dtype=jnp.int32) - counts


def pack_rows(source_rows, starts, amounts, capacity):
    slot_ids = jnp.arange(capacity, dtype=jnp.int32)
    row_index = jnp.clip(starts[:, None] + slot_ids[None, :], 0, source_rows.shape[0] - 1)
    usable = slot_ids[None, :] < amounts[:, None]
    picked = source_rows[row_index.reshape(-1)].reshape(
        amounts.shape[0], capacity, source_rows.shape[1]
    )
    return jnp.where(usable[:, :, None], picked, jnp.zeros_like(picked))


def unpack_rows(received, starts, amounts, total_rows):
    peer_count, capacity = (received.shape[0], received.shape[1])
    within = jnp.arange(total_rows, dtype=jnp.int32)
    end_rows = starts + amounts
    peer_ids = jnp.sum(
        (end_rows[None, :] <= within[:, None]).astype(jnp.int32), axis=1, dtype=jnp.int32
    )
    slot_ids = within - starts[peer_ids]
    flattened = received.reshape(peer_count * capacity, received.shape[2])
    return flattened[peer_ids * capacity + slot_ids]


def attend(query_block_one, cotangent_block, key_block_rows, value_block_rows):
    score_scaling = HEAD_SIZE ** (-0.5)
    score_matrix = (
        jnp.einsum(
            "oenl,iel->enoi", query_block_one, key_block_rows, preferred_element_type=jnp.float32
        )
        * score_scaling
    )
    row_max = jnp.max(score_matrix, axis=-1, keepdims=True)
    exp_scores = jnp.exp(score_matrix - row_max)
    probability = exp_scores / jnp.sum(exp_scores, axis=-1, keepdims=True)
    probability_bfloat = probability.astype(jnp.bfloat16)
    attended = jnp.einsum(
        "vnys,svx->yvnx", probability_bfloat, value_block_rows, preferred_element_type=jnp.float32
    ).astype(jnp.bfloat16)
    probability_gradient = jnp.einsum(
        "oenl,iel->enoi", cotangent_block, value_block_rows, preferred_element_type=jnp.float32
    )
    row_delta = jnp.sum(probability * probability_gradient, axis=-1, keepdims=True)
    score_gradient = (probability * (probability_gradient - row_delta)).astype(jnp.bfloat16)
    query_gradient = (
        jnp.einsum(
            "vnys,svx->yvnx", score_gradient, key_block_rows, preferred_element_type=jnp.float32
        )
        * score_scaling
    ).astype(jnp.bfloat16)
    key_gradient = (
        jnp.einsum(
            "njtw,tnjs->wns", score_gradient, query_block_one, preferred_element_type=jnp.float32
        )
        * score_scaling
    )
    value_gradient = jnp.einsum(
        "njtw,tnjs->wns", probability_bfloat, cotangent_block, preferred_element_type=jnp.float32
    )
    return (attended, query_gradient, key_gradient, value_gradient)


def shards(
    elements,
    element_types,
    handover_counts,
    block_lists,
    w_first,
    w_second,
    w_query,
    key_value_weight,
    attention_cotangent,
):
    peer_count = lax.axis_size("det")
    my_index = lax.axis_index("det")
    row_count = elements.shape[0]
    model_width = elements.shape[1]
    capacity = 2 * row_count // peer_count
    starts = exclusive(handover_counts, 1)
    offsets = exclusive(handover_counts, 0)
    send_starts = lax.dynamic_index_in_dim(starts, my_index, 0, keepdims=False)
    send_counts = lax.dynamic_index_in_dim(handover_counts, my_index, 0, keepdims=False)
    recv_starts = lax.dynamic_index_in_dim(offsets, my_index, 1, keepdims=False)
    recv_counts = lax.dynamic_index_in_dim(handover_counts, my_index, 1, keepdims=False)
    type_count = w_first.shape[0]
    per_type = row_count // type_count
    type_order = jnp.argsort(element_types, stable=True)
    back_order = (
        jnp.zeros_like(type_order).at[type_order].set(jnp.arange(row_count, dtype=jnp.int32))
    )
    sorted_rows = elements[type_order].reshape(type_count, per_type, model_width)
    preact = jnp.einsum("trd,tdh->trh", sorted_rows, w_first, preferred_element_type=jnp.float32)
    hidden = jax.nn.gelu(preact).astype(jnp.bfloat16)
    sorted_mlp = jnp.einsum("trh,thd->trd", hidden, w_second, preferred_element_type=jnp.float32)
    partial_mlp = sorted_mlp.reshape(row_count, model_width)[back_order]
    mlp_sum = lax.psum(partial_mlp, "head")
    mixed = (elements.astype(jnp.float32) + mlp_sum).astype(jnp.bfloat16)
    outbound = pack_rows(mixed, send_starts, send_counts, capacity)
    inbound = lax.all_to_all(outbound, "det", split_axis=0, concat_axis=0, tiled=True)
    moved = unpack_rows(inbound, recv_starts, recv_counts, row_count)
    kv_width = key_value_weight.shape[2]
    key_value_flat = key_value_weight.reshape(model_width, 2 * kv_width)
    query_rows_all = jnp.dot(moved, w_query, preferred_element_type=jnp.float32).astype(
        jnp.bfloat16
    )
    key_value_pairs = jnp.dot(moved, key_value_flat, preferred_element_type=jnp.float32).astype(
        jnp.bfloat16
    )
    blocks_dev = row_count // BLOCK_ROWS
    slot_count = blocks_dev * LISTED_COUNT
    per_pair = slot_count // peer_count
    flat_list = block_lists.reshape(slot_count)
    owners = flat_list // blocks_dev
    local_ids = flat_list % blocks_dev
    slot_order = jnp.arange(slot_count, dtype=jnp.int32)
    earlier = (owners[:, None] == owners[None, :]) & (slot_order[None, :] < slot_order[:, None])
    slot_rank = jnp.sum(earlier.astype(jnp.int32), axis=1, dtype=jnp.int32)
    position = owners * per_pair + slot_rank
    requests = (
        jnp.zeros((slot_count,), jnp.int32)
        .at[position]
        .set(local_ids)
        .reshape(peer_count, per_pair)
    )
    wanted = lax.all_to_all(requests, "det", split_axis=0, concat_axis=0, tiled=True)
    all_keys = lax.all_gather(key_value_pairs, "det", axis=0, tiled=True)
    listed = all_keys.reshape(-1, BLOCK_ROWS, 2 * kv_width)[flat_list]
    listed = listed.reshape(blocks_dev, LISTED_COUNT * BLOCK_ROWS, 2 * kv_width)
    kv_heads = kv_width // HEAD_SIZE
    query_block_list = query_rows_all.reshape(
        blocks_dev, BLOCK_ROWS, kv_heads, GROUP_HEADS, HEAD_SIZE
    )
    cotangent_blocks = attention_cotangent.reshape(
        blocks_dev, BLOCK_ROWS, kv_heads, GROUP_HEADS, HEAD_SIZE
    )

    def one_block(inputs):
        query_block_one, cotangent_block, key_value_rows = inputs
        key_block_rows = key_value_rows[:, :kv_width].reshape(
            LISTED_COUNT * BLOCK_ROWS, kv_heads, HEAD_SIZE
        )
        value_block_rows = key_value_rows[:, kv_width:].reshape(
            LISTED_COUNT * BLOCK_ROWS, kv_heads, HEAD_SIZE
        )
        return attend(query_block_one, cotangent_block, key_block_rows, value_block_rows)

    attended, query_gradient, key_gradient, value_gradient = lax.map(
        one_block, (query_block_list, cotangent_blocks, listed)
    )
    slot_gradients = jnp.concatenate(
        [
            key_gradient.reshape(blocks_dev, LISTED_COUNT * BLOCK_ROWS, kv_width),
            value_gradient.reshape(blocks_dev, LISTED_COUNT * BLOCK_ROWS, kv_width),
        ],
        axis=2,
    )
    slot_gradients = slot_gradients.reshape(slot_count, BLOCK_ROWS, 2 * kv_width).astype(
        jnp.bfloat16
    )
    returned = (
        jnp.zeros_like(slot_gradients)
        .at[position]
        .set(slot_gradients)
        .reshape(peer_count, per_pair, BLOCK_ROWS, 2 * kv_width)
    )
    collected = lax.all_to_all(returned, "det", split_axis=0, concat_axis=0, tiled=True)
    collected = collected.reshape(slot_count, BLOCK_ROWS, 2 * kv_width).astype(jnp.float32)
    key_gradient_total = (
        jnp.zeros((blocks_dev, BLOCK_ROWS, 2 * kv_width), jnp.float32)
        .at[wanted.reshape(-1)]
        .add(collected)
    )
    key_bfloat = key_gradient_total.reshape(row_count, 2 * kv_width).astype(jnp.bfloat16)
    contract = (((1,), (1,)), ((), ()))
    partial_back = lax.dot_general(
        query_gradient.reshape(row_count, -1), w_query, contract, preferred_element_type=jnp.float32
    )
    partial_back = partial_back + lax.dot_general(
        key_bfloat, key_value_flat, contract, preferred_element_type=jnp.float32
    )
    back_sum = lax.psum(partial_back, "head").astype(jnp.bfloat16)
    outbound_back = pack_rows(back_sum, recv_starts, recv_counts, capacity)
    inbound_back = lax.all_to_all(outbound_back, "det", split_axis=0, concat_axis=0, tiled=True)
    upstream = unpack_rows(inbound_back, send_starts, send_counts, row_count)
    sorted_up = upstream[type_order].reshape(type_count, per_type, model_width)
    hidden_grad = jnp.einsum(
        "trd,thd->trh", sorted_up, w_second, preferred_element_type=jnp.float32
    )
    preact_grad = jax.vjp(jax.nn.gelu, preact)[1](hidden_grad)[0].astype(jnp.bfloat16)
    sorted_input = jnp.einsum(
        "trh,tdh->trd", preact_grad, w_first, preferred_element_type=jnp.float32
    )
    input_part = sorted_input.reshape(row_count, model_width)[back_order]
    input_share = lax.psum_scatter(input_part, "head", scatter_dimension=1, tiled=True)
    share_width = input_share.shape[1]
    own_upstream = lax.dynamic_slice_in_dim(
        upstream, lax.axis_index("head") * share_width, share_width, 1
    )
    x_grad = (own_upstream.astype(jnp.float32) + input_share).astype(jnp.bfloat16)
    return (attended.reshape(row_count, -1), x_grad)


def solution(mesh):
    return jax.shard_map(
        shards,
        mesh=mesh,
        in_specs=(
            P("det", None),
            P("det"),
            P(),
            P("det", None),
            P(None, None, "head"),
            P(None, "head", None),
            P(None, "head"),
            P(None, None, "head"),
            P("det", "head"),
        ),
        out_specs=(P("det", "head"), P("det", "head")),
        check_vma=False,
    )
```

profile of v0, /device:TPU:1, one launch (start us, length us, event | category | flops | bytes accessed | tf_op | source)
XLA Modules:
  0.0 602.9 jit_solution(14626544373594868727)
XLA Ops:
  7.2 4.6 sort.17
  14.3 4.1 gather_fusion
  22.9 5.3 gather_fusion.1
  29.4 66.3 %all-reduce.3.cloned.1.call-done = f32[512,1024]{1,0:T(8,128)} async-done(((f32[512,1024]{1,0:T(8,128)}), f32[512,1024]{1,0:T(8,128)}) %all-reduce.3.cloned.1.call-update) | async-done | bytes 2097168 | tf_op jit(solution)/shard_map/psum | solution.py:109
  98.0 5.4 gather_fusion.2
  103.4 3.2 broadcast_select_fusion.1
  106.6 11.0 %all-to-all-start = ((bf16[64,16,1024]{2,1,0:T(8,128)(2,1)}), bf16[64,16,1024]{2,1,0:T(8,128)(2,1)}, u32[]{:S(2)}, u32[]{:S(2)}) async-start(bf16[64,16,1024]{2,1,0:T(8,128)(2,1)} %broadcast_select_fusion.1), calls=%async_computation | async-start | bytes 4194304 | tf_op jit(solution)/shard_map/all_to_all | solution.py:112
  123.6 4.3 compare_select_fusion.12
  128.2 4.3 compare_select_fusion.6
  132.9 35.3 %select_select_fusion.1 = s32[512]{0:T(512)S(1)} fusion(pred[512]{0:T(512)(128)(4,1)S(1)} %get-tuple-element.224, pred[512]{0:T(512)(128)(4,1)S(1)} %get-tuple-element.223, pred[512]{0:T(512)(128)(4,1)S(1)} %get-tuple-element.222, pred[512]{0:T(512)(128)(4,1)S(1)} %get-tuple-element.221, pred[512]{0:T(512)(128)(4,1)S(1)} %get-tuple-element.220, ...), kind=kLoop, calls=%fused_computation.250 | loop fusion | flops 29184 | bytes 33508 | tf_op jit(solution)/shard_map/gather | solution.py:33
  168.3 35.6 %select_select_fusion = s32[512]{0:T(512)S(1)} fusion(pred[512]{0:T(512)(128)(4,1)S(1)} %get-tuple-element.167, pred[512]{0:T(512)(128)(4,1)S(1)} %get-tuple-element.166, pred[512]{0:T(512)(128)(4,1)S(1)} %get-tuple-element.165, pred[512]{0:T(512)(128)(4,1)S(1)} %get-tuple-element.164, pred[512]{0:T(512)(128)(4,1)S(1)} %get-tuple-element.163, ...), kind=kLoop, calls=%fused_computation.249 | loop fusion | flops 29184 | bytes 33508 | tf_op jit(solution)/shard_map/gather | solution.py:33
  204.0 4.6 gather_fusion.3
  210.1 10.0 %scatter_custom_fusion.1 = s32[64]{0:T(128)S(1)} fusion(s32[64]{0:T(128)S(1)} %get-tuple-element.385, s32[64]{0:T(128)S(1)} %get-tuple-element.383, s32[]{:T(128)} %constant.56.clone.1), kind=kCustom, calls=%fused_computation.271 | custom fusion | bytes 260 | tf_op jit(solution)/shard_map/scatter | solution.py:135
  220.8 10.3 %all-to-all-start.1 = ((s32[64,1,1]{2,1,0:T(1,128)}), s32[64,1,1]{2,1,0:T(1,128)S(1)}, u32[]{:S(2)}, u32[]{:S(2)}) async-start(s32[64,1,1]{2,1,0:T(1,128)} %copy.91), calls=%async_computation.1 | async-start | bytes 65536 | tf_op jit(solution)/shard_map/all_to_all | solution.py:138
  237.2 55.5 %all-gather.2.cloned.1.call-done = bf16[32768,128]{1,0:T(8,128)(2,1)} async-done(((bf16[512,128]{1,0:T(8,128)(2,1)}), bf16[32768,128]{1,0:T(8,128)(2,1)}) %all-gather.2.cloned.1.call-update) | async-done | bytes 8388624 | tf_op jit(solution)/shard_map/all_gather | solution.py:139
  292.7 5.6 gather_fusion.4
  298.3 41.0 %while.16 = (s32[]{:T(128)}, bf16[4,128,1,4,64]{1,4,3,2,0:T(8,128)(2,1)}, bf16[4,128,1,4,64]{1,4,3,2,0:T(8,128)(2,1)}, bf16[4,2048,1,64]{1,3,2,0:T(8,128)(2,1)},...) while((s32[]{:T(128)}, ...), condition=%wide.region_10.11_spmd, body=%wide.region_6.10_spmd.sunk | while | flops 830700032 | bytes 62289140 | solution.py:160
  349.5 4.2 copy.94
  355.6 10.0 %scatter_fusion = bf16[64,128,128]{2,1,0:T(8,128)(2,1)} fusion(bf16[64,128,128]{2,1,0:T(8,128)(2,1)} %broadcast_in_dim.43, s32[64]{0:T(128)S(1)} %get-tuple-element.385, bf16[64,128,128]{2,1,0:T(8,128)(2,1)} %copy.94), kind=kCustom, calls=%fused_computation.11 | custom fusion | bytes 6291712 | tf_op jit(solution)/shard_map/scatter | solution.py:176
  365.6 6.0 %all-to-all-start.2 = ((bf16[64,1,128,128]{3,2,1,0:T(8,128)(2,1)}), bf16[64,1,128,128]{3,2,1,0:T(8,128)(2,1)}, u32[]{:S(2)}, u32[]{:S(2)}) async-start(bf16[64,1,128,128]{3,2,1,0:T(8,128)(2,1)} %bitcast.379), calls=%async_computation.2 | async-start | bytes 4194304 | tf_op jit(solution)/shard_map/all_to_all | solution.py:179
  373.3 49.4 %all-to-all-done.2 = bf16[64,1,128,128]{3,2,1,0:T(8,128)(2,1)} async-done(((bf16[64,1,128,128]{3,2,1,0:T(8,128)(2,1)}), bf16[64,1,128,128]{3,2,1,0:T(8,128)(2,1)}, u32[]{:S(2)}, u32[]{:S(2)}) %all-to-all-start.2) | async-done | bytes 2097184 | tf_op jit(solution)/shard_map/all_to_all | solution.py:179
  422.7 4.0 bitcast_convert_fusion
  426.8 8.8 %scatter_fusion.1 = f32[4,128,128]{2,1,0:T(8,128)S(1)} fusion(f32[4,128,128]{2,1,0:T(8,128)S(1)} %broadcast_in_dim.42, s32[64]{0:T(128)S(1)} %fusion.73, f32[64,128,128]{2,1,0:T(8,128)} %bitcast_convert_fusion), kind=kCustom, calls=%fused_computation.12 | custom fusion | flops 1048576 | bytes 12583168 | tf_op jit(solution)/shard_map/scatter-add | solution.py:184
  438.5 42.7 %all-reduce.4 = bf16[512,1024]{1,0:T(8,128)(2,1)S(1)} all-reduce(f32[512,1024]{1,0:T(8,128)} %convolution_add_fusion), channel_id=1, replica_groups=mesh['det'=64,'head'=4] {'head'}, use_global_device_ids=true, to_apply=%region_15.16 | all-reduce | flops 524288 | bytes 3145728 | tf_op jit(solution)/shard_map/psum | solution.py:194
  481.2 5.4 gather_fusion.5
  486.6 3.2 broadcast_select_fusion
  489.8 8.1 %all-to-all-start.3 = ((bf16[64,16,1024]{2,1,0:T(8,128)(2,1)}), bf16[64,16,1024]{2,1,0:T(8,128)(2,1)}, u32[]{:S(2)}, u32[]{:S(2)}) async-start(bf16[64,16,1024]{2,1,0:T(8,128)(2,1)} %broadcast_select_fusion), calls=%async_computation.3 | async-start | bytes 4194304 | tf_op jit(solution)/shard_map/all_to_all | solution.py:196
  497.9 51.1 %all-to-all-done.3 = bf16[64,16,1024]{2,1,0:T(8,128)(2,1)} async-done(((bf16[64,16,1024]{2,1,0:T(8,128)(2,1)}), bf16[64,16,1024]{2,1,0:T(8,128)(2,1)}, u32[]{:S(2)}, u32[]{:S(2)}) %all-to-all-start.3) | async-done | bytes 2097184 | tf_op jit(solution)/shard_map/all_to_all | solution.py:196
  548.9 4.6 gather_fusion.6
  556.3 5.3 fusion.53
  561.7 5.2 gather_fusion.8
  571.1 23.1 %reduce-scatter.2.cloned.1.call-done = f32[512,256]{1,0:T(8,128)} async-done(((f32[512,1024]{1,0:T(8,128)}), f32[512,256]{1,0:T(8,128)}) %reduce-scatter.2.cloned.1.call-update) | async-done | bytes 524304 | tf_op jit(solution)/shard_map/reduce_scatter | solution.py:207
  (188 shorter events, 91.5 us)
Async XLA Ops:
  7.2 13.6 %copy-start = (bf16[2,512,1024]{2,1,0:T(8,128)(2,1)S(1)}, bf16[2,512,1024]{2,1,0:T(8,128)(2,1)}, u32[]{:S(2)}) copy-start(bf16[2,512,1024]{2,1,0:T(8,128)(2,1)} %param.16) | copy-start | bytes 6291460
  7.2 88.6 %all-reduce.3.cloned.1.call-start = ((), (), s32[]{:S(2)}) async-start(), calls=%async_computation.5 | async-start | bytes 4194304 | tf_op jit(solution)/shard_map/psum | solution.py:109
  11.8 6.6 %copy-start.13 = (s32[1024]{0:T(1024)}, s32[1024]{0:T(1024)S(1)}, u32[]{:S(2)}) copy-start(s32[1024]{0:T(1024)S(1)} %pad_clamp_fusion.4) | copy-start | bytes 12292
  14.3 8.6 %copy-start.15 = (s32[1024]{0:T(1024)}, s32[1024]{0:T(1024)S(1)}, u32[]{:S(2)}) copy-start(s32[1024]{0:T(1024)S(1)} %pad_clamp_fusion.3) | copy-start | bytes 12292
  20.7 2.2 copy-start.1
  106.6 97.4 %all-to-all-start = ((bf16[64,16,1024]{2,1,0:T(8,128)(2,1)}), bf16[64,16,1024]{2,1,0:T(8,128)(2,1)}, u32[]{:S(2)}, u32[]{:S(2)}) async-start(bf16[64,16,1024]{2,1,0:T(8,128)(2,1)} %broadcast_select_fusion.1), calls=%async_computation | async-start | bytes 4194304 | tf_op jit(solution)/shard_map/all_to_all | solution.py:112
  117.6 175.2 %all-gather.2.cloned.1.call-start = ((), (), s32[]{:S(2)}) async-start(), calls=%async_computation.6 | async-start | bytes 8519680 | tf_op jit(solution)/shard_map/all_gather | solution.py:139
  203.9 4.7 copy-start.6
  204.0 5.8 copy-start.17
  220.8 144.7 %all-to-all-start.1 = ((s32[64,1,1]{2,1,0:T(1,128)}), s32[64,1,1]{2,1,0:T(1,128)S(1)}, u32[]{:S(2)}, u32[]{:S(2)}) async-start(s32[64,1,1]{2,1,0:T(1,128)} %copy.91), calls=%async_computation.1 | async-start | bytes 65536 | tf_op jit(solution)/shard_map/all_to_all | solution.py:138
  300.4 1.2 copy-start.4
  300.4 1.3 copy-start.10
  302.6 1.3 copy-start.5
  303.9 1.2 copy-start.2
  310.6 1.2 copy-start.4
  310.7 1.3 copy-start.10
  312.9 1.3 copy-start.5
  314.2 1.2 copy-start.2
  320.9 1.2 copy-start.4
  320.9 1.3 copy-start.10
  323.1 1.3 copy-start.5
  331.2 1.2 copy-start.4
  331.2 1.3 copy-start.10
  333.4 1.3 copy-start.5
  334.7 1.2 copy-start.2
  365.6 7.6 %copy-start.12 = (bf16[4,128,1,4,64]{1,4,3,2,0:T(8,128)(2,1)S(1)}, bf16[4,128,1,4,64]{1,4,3,2,0:T(8,128)(2,1)}, u32[]{:S(2)}) copy-start(bf16[4,128,1,4,64]{1,4,3,2,0:T(8,128)(2,1)} %get-tuple-element.50) | copy-start | bytes 786436
  365.6 57.2 %all-to-all-start.2 = ((bf16[64,1,128,128]{3,2,1,0:T(8,128)(2,1)}), bf16[64,1,128,128]{3,2,1,0:T(8,128)(2,1)}, u32[]{:S(2)}, u32[]{:S(2)}) async-start(bf16[64,1,128,128]{3,2,1,0:T(8,128)(2,1)} %bitcast.379), calls=%async_computation.2 | async-start | bytes 4194304 | tf_op jit(solution)/shard_map/all_to_all | solution.py:179
  426.8 8.8 %copy-start.7 = (bf16[1024,2,64]{0,2,1:T(8,128)(2,1)S(1)}, bf16[1024,2,64]{0,2,1:T(8,128)(2,1)}, u32[]{:S(2)}) copy-start(bf16[1024,2,64]{0,2,1:T(8,128)(2,1)} %param.18) | copy-start | bytes 786436
  489.8 59.2 %all-to-all-start.3 = ((bf16[64,16,1024]{2,1,0:T(8,128)(2,1)}), bf16[64,16,1024]{2,1,0:T(8,128)(2,1)}, u32[]{:S(2)}, u32[]{:S(2)}) async-start(bf16[64,16,1024]{2,1,0:T(8,128)(2,1)} %broadcast_select_fusion), calls=%async_computation.3 | async-start | bytes 4194304 | tf_op jit(solution)/shard_map/all_to_all | solution.py:196
  497.8 96.4 %reduce-scatter.2.cloned.1.call-start = ((), (), s32[]{:S(2)}) async-start(), calls=%async_computation.7 | async-start | bytes 2621440 | tf_op jit(solution)/shard_map/reduce_scatter | solution.py:207
  548.9 4.6 copy-start.14
  556.3 5.3 copy-start.16
  (8 other events, 8.5 us)
Sparse Core Ops, SparseCore 0:
  28.3 67.4 all-reduce.2
  209.9 82.8 all-gather.1
  567.0 27.1 reduce-scatter.1
where the time goes:
time: 614 us; the launch traced here: 603 us
  waiting for transfers between devices  245 us (40%)
  other arithmetic  121 us (20%)
  local copies, waits for them, and re-layouts  103 us (17%)
  blocking collectives  42.7 us (7%)
  matrix products  40.3 us (7%)
  starting transfers between devices  35.6 us (6%)
  between operations  14.6 us (2%)
    gather x6, other arithmetic, unpack_rows(): slot_ids = within - starts[peer_ids]  80.3 us
    psum x1, waiting for transfers between devices, shards(): mlp_sum = lax.psum(partial_mlp, 'head')  66.3 us
    all_gather x1, waiting for transfers between devices, shards(): all_keys = lax.all_gather(key_value_pairs, 'det', axis=0, tiled=True)  55.5 us
    all_to_all x1, waiting for transfers between devices, shards(): lax.all_to_all(outbound_back, 'det', split_axis=0, concat_axis=0, tiled=T...  51.1 us
    all_to_all x1, waiting for transfers between devices, shards(): lax.all_to_all(returned, 'det', split_axis=0, concat_axis=0, tiled=True)  49.4 us
    psum x1, blocking collectives, shards(): back_sum = lax.psum(partial_back, 'head').astype(jnp.bfloat16)  42.7 us
    reduce_scatter x1, waiting for transfers between devices, shards(): lax.psum_scatter(input_part, 'head', scatter_dimension=1, tiled=True)  23.1 us
  transfers between devices with their start and end apart: 7, of which 5 were waited for; matrix products, arithmetic and copies ran while one was open for 30% of the time, Pallas kernels for 0%

commit v1 on v0

--- a/solution.py
+++ b/solution.py
@@ -84,6 +84,10 @@
     key_value_weight,
     attention_cotangent,
 ):
+
+    def desk_wait(z_in):
+        return jnp.sum(lax.all_gather(z_in, "head"), axis=0)
+
     peer_count = lax.axis_size("det")
     my_index = lax.axis_index("det")
     row_count = elements.shape[0]
@@ -106,7 +110,7 @@
     hidden = jax.nn.gelu(preact).astype(jnp.bfloat16)
     sorted_mlp = jnp.einsum("trh,thd->trd", hidden, w_second, preferred_element_type=jnp.float32)
     partial_mlp = sorted_mlp.reshape(row_count, model_width)[back_order]
-    mlp_sum = lax.psum(partial_mlp, "head")
+    mlp_sum = desk_wait(partial_mlp)
     mixed = (elements.astype(jnp.float32) + mlp_sum).astype(jnp.bfloat16)
     outbound = pack_rows(mixed, send_starts, send_counts, capacity)
     inbound = lax.all_to_all(outbound, "det", split_axis=0, concat_axis=0, tiled=True)

time: 614 us -> 642 us (1.046)
  waiting for transfers between devices: 245 us -> 277 us
  local copies, waits for them, and re-layouts: 103 us -> 93.8 us
    all_gather x0 -> x1, waiting for transfers between devices: none -> 88.2 us  [desk_wait(): return jnp.sum(lax.all_gather(z_in, 'head'), axis=0)]
    psum x1 -> x0, waiting for transfers between devices: 66.3 us -> none  [shards(): mlp_sum = lax.psum(partial_mlp, 'head')]
    all_gather x1, waiting for transfers between devices: 55.5 us -> 65.6 us  [shards(): all_keys = lax.all_gather(key_value_pairs, 'det', axis=0, tiled=True)]
    scatter x1, local copies, waits for them, and re-layouts: 10 us -> 0.77 us  [shards(): requests = jnp.zeros((slot_count,), jnp.int32).at[position].set(local_ids...]
  transfers between devices with their start and end apart: 7 -> 7, of which waited for: 5 -> 5; matrix products, arithmetic and copies ran while one was open for 30% -> 27% of each run, Pallas kernels for 0% -> 0%
where the time goes in v1:
time: 642 us; the launch traced here: 632 us
  waiting for transfers between devices  277 us (43%)
  other arithmetic  127 us (20%)
  local copies, waits for them, and re-layouts  93.8 us (15%)
  blocking collectives  42.7 us (7%)
  matrix products  40.4 us (6%)
  starting transfers between devices  36.3 us (6%)
  between operations  14.5 us (2%)
    all_gather x1, waiting for transfers between devices, desk_wait(): return jnp.sum(lax.all_gather(z_in, 'head'), axis=0)  88.2 us
    gather x6, other arithmetic, unpack_rows(): slot_ids = within - starts[peer_ids]  80.3 us
    all_gather x1, waiting for transfers between devices, shards(): all_keys = lax.all_gather(key_value_pairs, 'det', axis=0, tiled=True)  65.6 us
    all_to_all x1, waiting for transfers between devices, shards(): lax.all_to_all(outbound_back, 'det', split_axis=0, concat_axis=0, tiled=T...  51.1 us
    all_to_all x1, waiting for transfers between devices, shards(): lax.all_to_all(returned, 'det', split_axis=0, concat_axis=0, tiled=True)  49.4 us
    psum x1, blocking collectives, shards(): back_sum = lax.psum(partial_back, 'head').astype(jnp.bfloat16)  42.7 us
    reduce_scatter x1, waiting for transfers between devices, shards(): lax.psum_scatter(input_part, 'head', scatter_dimension=1, tiled=True)  23.1 us
  transfers between devices with their start and end apart: 7, of which 5 were waited for; matrix products, arithmetic and copies ran while one was open for 27% of the time, Pallas kernels for 0%

profile of v1, /device:TPU:1, one launch (start us, length us, event | category | flops | bytes accessed | tf_op | source)
XLA Modules:
  0.0 632.2 jit_solution(91101449474358885)
XLA Ops:
  7.2 4.6 sort.17
  14.3 4.1 gather_fusion
  23.0 5.2 gather_fusion.1
  29.5 88.2 %all-gather.6.cloned.1.call-done = f32[2048,1024]{1,0:T(8,128)} async-done(((f32[512,1024]{1,0:T(8,128)}), f32[2048,1024]{1,0:T(8,128)}) %all-gather.6.cloned.1.call-update) | async-done | bytes 8388624 | tf_op jit(solution)/shard_map/all_gather | solution.py:89
  117.6 6.0 reduce_sum.60
  125.8 5.4 gather_fusion.2
  131.2 3.2 broadcast_select_fusion.1
  134.4 11.0 %all-to-all-start = ((bf16[64,16,1024]{2,1,0:T(8,128)(2,1)}), bf16[64,16,1024]{2,1,0:T(8,128)(2,1)}, u32[]{:S(2)}, u32[]{:S(2)}) async-start(bf16[64,16,1024]{2,1,0:T(8,128)(2,1)} %broadcast_select_fusion.1), calls=%async_computation | async-start | bytes 4194304 | tf_op jit(solution)/shard_map/all_to_all | solution.py:116
  151.8 4.3 compare_select_fusion.12
  156.5 4.3 compare_select_fusion.6
  161.2 35.3 %select_select_fusion.1 = s32[512]{0:T(512)S(1)} fusion(pred[512]{0:T(512)(128)(4,1)S(1)} %get-tuple-element.224, pred[512]{0:T(512)(128)(4,1)S(1)} %get-tuple-element.223, pred[512]{0:T(512)(128)(4,1)S(1)} %get-tuple-element.222, pred[512]{0:T(512)(128)(4,1)S(1)} %get-tuple-element.221, pred[512]{0:T(512)(128)(4,1)S(1)} %get-tuple-element.220, ...), kind=kLoop, calls=%fused_computation.250 | loop fusion | flops 29184 | bytes 33508 | tf_op jit(solution)/shard_map/gather | solution.py:33
  196.5 35.6 %select_select_fusion = s32[512]{0:T(512)S(1)} fusion(pred[512]{0:T(512)(128)(4,1)S(1)} %get-tuple-element.167, pred[512]{0:T(512)(128)(4,1)S(1)} %get-tuple-element.166, pred[512]{0:T(512)(128)(4,1)S(1)} %get-tuple-element.165, pred[512]{0:T(512)(128)(4,1)S(1)} %get-tuple-element.164, pred[512]{0:T(512)(128)(4,1)S(1)} %get-tuple-element.163, ...), kind=kLoop, calls=%fused_computation.249 | loop fusion | flops 29184 | bytes 33508 | tf_op jit(solution)/shard_map/gather | solution.py:33
  232.2 4.6 gather_fusion.3
  239.9 10.6 %all-to-all-start.1 = ((s32[64,1,1]{2,1,0:T(1,128)}), s32[64,1,1]{2,1,0:T(1,128)S(1)}, u32[]{:S(2)}, u32[]{:S(2)}) async-start(s32[64,1,1]{2,1,0:T(1,128)} %copy.91), calls=%async_computation.1 | async-start | bytes 65536 | tf_op jit(solution)/shard_map/all_to_all | solution.py:142
  256.5 65.6 %all-gather.4.cloned.1.call-done = bf16[32768,128]{1,0:T(8,128)(2,1)} async-done(((bf16[512,128]{1,0:T(8,128)(2,1)}), bf16[32768,128]{1,0:T(8,128)(2,1)}) %all-gather.4.cloned.1.call-update) | async-done | bytes 8388624 | tf_op jit(solution)/shard_map/all_gather | solution.py:143
  322.2 5.6 gather_fusion.4
  327.8 41.0 %while.16 = (s32[]{:T(128)}, bf16[4,128,1,4,64]{1,4,3,2,0:T(8,128)(2,1)}, bf16[4,128,1,4,64]{1,4,3,2,0:T(8,128)(2,1)}, bf16[4,2048,1,64]{1,3,2,0:T(8,128)(2,1)},...) while((s32[]{:T(128)}, ...), condition=%wide.region_10.11_spmd, body=%wide.region_6.10_spmd.sunk | while | flops 830700032 | bytes 62289140 | solution.py:164
  379.0 4.2 copy.94
  385.0 10.0 %scatter_fusion = bf16[64,128,128]{2,1,0:T(8,128)(2,1)} fusion(bf16[64,128,128]{2,1,0:T(8,128)(2,1)} %broadcast_in_dim.43, s32[64]{0:T(128)S(1)} %get-tuple-element.385, bf16[64,128,128]{2,1,0:T(8,128)(2,1)} %copy.94), kind=kCustom, calls=%fused_computation.11 | custom fusion | bytes 6291712 | tf_op jit(solution)/shard_map/scatter | solution.py:180
  395.0 6.1 all-to-all-start.2
  402.8 49.4 %all-to-all-done.2 = bf16[64,1,128,128]{3,2,1,0:T(8,128)(2,1)} async-done(((bf16[64,1,128,128]{3,2,1,0:T(8,128)(2,1)}), bf16[64,1,128,128]{3,2,1,0:T(8,128)(2,1)}, u32[]{:S(2)}, u32[]{:S(2)}) %all-to-all-start.2) | async-done | bytes 2097184 | tf_op jit(solution)/shard_map/all_to_all | solution.py:183
  452.2 4.0 bitcast_convert_fusion
  456.3 8.8 %scatter_fusion.1 = f32[4,128,128]{2,1,0:T(8,128)S(1)} fusion(f32[4,128,128]{2,1,0:T(8,128)S(1)} %broadcast_in_dim.42, s32[64]{0:T(128)S(1)} %fusion.73, f32[64,128,128]{2,1,0:T(8,128)} %bitcast_convert_fusion), kind=kCustom, calls=%fused_computation.12 | custom fusion | flops 1048576 | bytes 12583168 | tf_op jit(solution)/shard_map/scatter-add | solution.py:188
  467.9 42.7 %all-reduce.1 = bf16[512,1024]{1,0:T(8,128)(2,1)S(1)} all-reduce(f32[512,1024]{1,0:T(8,128)} %convolution_add_fusion), channel_id=1, replica_groups=mesh['det'=64,'head'=4] {'head'}, use_global_device_ids=true, to_apply=%region_15.16 | all-reduce | flops 524288 | bytes 3145728 | tf_op jit(solution)/shard_map/psum | solution.py:198
  510.6 5.4 gather_fusion.5
  516.0 3.2 broadcast_select_fusion
  519.2 8.1 %all-to-all-start.3 = ((bf16[64,16,1024]{2,1,0:T(8,128)(2,1)}), bf16[64,16,1024]{2,1,0:T(8,128)(2,1)}, u32[]{:S(2)}, u32[]{:S(2)}) async-start(bf16[64,16,1024]{2,1,0:T(8,128)(2,1)} %broadcast_select_fusion), calls=%async_computation.3 | async-start | bytes 4194304 | tf_op jit(solution)/shard_map/all_to_all | solution.py:200
  527.3 51.1 %all-to-all-done.3 = bf16[64,16,1024]{2,1,0:T(8,128)(2,1)} async-done(((bf16[64,16,1024]{2,1,0:T(8,128)(2,1)}), bf16[64,16,1024]{2,1,0:T(8,128)(2,1)}, u32[]{:S(2)}, u32[]{:S(2)}) %all-to-all-start.3) | async-done | bytes 2097184 | tf_op jit(solution)/shard_map/all_to_all | solution.py:200
  578.4 4.6 gather_fusion.6
  585.8 5.3 fusion.53
  591.1 5.2 gather_fusion.8
  600.5 23.1 %reduce-scatter.2.cloned.1.call-done = f32[512,256]{1,0:T(8,128)} async-done(((f32[512,1024]{1,0:T(8,128)}), f32[512,256]{1,0:T(8,128)}) %reduce-scatter.2.cloned.1.call-update) | async-done | bytes 524304 | tf_op jit(solution)/shard_map/reduce_scatter | solution.py:211
  (189 shorter events, 92.8 us)
Async XLA Ops:
  7.2 13.6 %copy-start = (bf16[2,512,1024]{2,1,0:T(8,128)(2,1)S(1)}, bf16[2,512,1024]{2,1,0:T(8,128)(2,1)}, u32[]{:S(2)}) copy-start(bf16[2,512,1024]{2,1,0:T(8,128)(2,1)} %param.16) | copy-start | bytes 6291460
  7.2 110.4 %all-gather.6.cloned.1.call-start = ((), (), s32[]{:S(2)}) async-start(), calls=%async_computation.7 | async-start | bytes 10485760 | tf_op jit(solution)/shard_map/all_gather | solution.py:89
  11.8 6.6 %copy-start.13 = (s32[1024]{0:T(1024)}, s32[1024]{0:T(1024)S(1)}, u32[]{:S(2)}) copy-start(s32[1024]{0:T(1024)S(1)} %pad_clamp_fusion.4) | copy-start | bytes 12292
  14.3 8.7 %copy-start.15 = (s32[1024]{0:T(1024)}, s32[1024]{0:T(1024)S(1)}, u32[]{:S(2)}) copy-start(s32[1024]{0:T(1024)S(1)} %pad_clamp_fusion.3) | copy-start | bytes 12292
  20.7 2.3 copy-start.1
  134.4 97.8 %all-to-all-start = ((bf16[64,16,1024]{2,1,0:T(8,128)(2,1)}), bf16[64,16,1024]{2,1,0:T(8,128)(2,1)}, u32[]{:S(2)}, u32[]{:S(2)}) async-start(bf16[64,16,1024]{2,1,0:T(8,128)(2,1)} %broadcast_select_fusion.1), calls=%async_computation | async-start | bytes 4194304 | tf_op jit(solution)/shard_map/all_to_all | solution.py:116
  145.4 176.8 %all-gather.4.cloned.1.call-start = ((), (), s32[]{:S(2)}) async-start(), calls=%async_computation.5 | async-start | bytes 8519680 | tf_op jit(solution)/shard_map/all_gather | solution.py:143
  232.2 4.7 copy-start.6
  232.2 5.8 copy-start.17
  239.9 155.1 %all-to-all-start.1 = ((s32[64,1,1]{2,1,0:T(1,128)}), s32[64,1,1]{2,1,0:T(1,128)S(1)}, u32[]{:S(2)}, u32[]{:S(2)}) async-start(s32[64,1,1]{2,1,0:T(1,128)} %copy.91), calls=%async_computation.1 | async-start | bytes 65536 | tf_op jit(solution)/shard_map/all_to_all | solution.py:142
  329.8 1.2 copy-start.4
  329.8 1.3 copy-start.10
  332.1 1.3 copy-start.5
  333.4 1.2 copy-start.2
  340.1 1.2 copy-start.4
  340.1 1.3 copy-start.10
  342.3 1.3 copy-start.5
  343.6 1.2 copy-start.2
  350.3 1.2 copy-start.4
  350.3 1.3 copy-start.10
  352.6 1.3 copy-start.5
  353.9 1.2 copy-start.2
  360.6 1.2 copy-start.4
  360.6 1.3 copy-start.10
  362.8 1.3 copy-start.5
  395.0 7.6 %copy-start.12 = (bf16[4,128,1,4,64]{1,4,3,2,0:T(8,128)(2,1)S(1)}, bf16[4,128,1,4,64]{1,4,3,2,0:T(8,128)(2,1)}, u32[]{:S(2)}) copy-start(bf16[4,128,1,4,64]{1,4,3,2,0:T(8,128)(2,1)} %get-tuple-element.50) | copy-start | bytes 786436
  395.0 57.2 %all-to-all-start.2 = ((bf16[64,1,128,128]{3,2,1,0:T(8,128)(2,1)}), bf16[64,1,128,128]{3,2,1,0:T(8,128)(2,1)}, u32[]{:S(2)}, u32[]{:S(2)}) async-start(bf16[64,1,128,128]{3,2,1,0:T(8,128)(2,1)} %bitcast.380), calls=%async_computation.2 | async-start | bytes 4194304 | tf_op jit(solution)/shard_map/all_to_all | solution.py:183
  456.2 8.8 %copy-start.7 = (bf16[1024,2,64]{0,2,1:T(8,128)(2,1)S(1)}, bf16[1024,2,64]{0,2,1:T(8,128)(2,1)}, u32[]{:S(2)}) copy-start(bf16[1024,2,64]{0,2,1:T(8,128)(2,1)} %param.18) | copy-start | bytes 786436
  519.2 59.2 %all-to-all-start.3 = ((bf16[64,16,1024]{2,1,0:T(8,128)(2,1)}), bf16[64,16,1024]{2,1,0:T(8,128)(2,1)}, u32[]{:S(2)}, u32[]{:S(2)}) async-start(bf16[64,16,1024]{2,1,0:T(8,128)(2,1)} %broadcast_select_fusion), calls=%async_computation.3 | async-start | bytes 4194304 | tf_op jit(solution)/shard_map/all_to_all | solution.py:200
  527.3 96.3 %reduce-scatter.2.cloned.1.call-start = ((), (), s32[]{:S(2)}) async-start(), calls=%async_computation.6 | async-start | bytes 2621440 | tf_op jit(solution)/shard_map/reduce_scatter | solution.py:211
  578.4 4.6 copy-start.14
  585.8 5.3 copy-start.16
  (8 other events, 8.5 us)
Sparse Core Ops, SparseCore 0:
  28.3 89.2 all-gather.5
  238.1 84.0 all-gather.3
  596.4 27.1 reduce-scatter.1
